TPU v7x, 32 devices: a whole 2x2x4 slice. The times are simulated.
32 devices in a mesh: dp: 8 (over z, x), seq: 4 (over y, core).
Axes of the slice: x: 2, y: 2, z: 4, core: 2. Of those that a mesh axis runs over, the one named last changes fastest.
Arguments:
- tokens: bfloat16 [16384, 1024], P(('dp', 'seq')), may hold values from -6 to 6
- out_grad: bfloat16 [16384, 1024], P(('dp', 'seq')), may hold values from -6 to 6
- qkv_weight: bfloat16 [1024, 3072], P('dp'), may hold values from -0.25 to 0.25
- qv_bias: bfloat16 [2, 1024], P(None, 'dp'), may hold values from -3 to 3
- proj_weight: bfloat16 [1024, 1024], P('dp'), may hold values from -0.1875 to 0.1875
- fc1_weight: bfloat16 [1024, 4096], P('dp'), may hold values from -0.1875 to 0.1875
- fc1_bias: bfloat16 [4096], P('dp'), may hold values from -3 to 3
- fc2_weight: bfloat16 [4096, 1024], P('dp'), may hold values from -0.09375 to 0.09375
- out_bias: bfloat16 [2, 1024], P(None, 'dp'), may hold values from -3 to 3
- norm_gains: bfloat16 [4, 1024], P(None, 'dp'), may hold values from 0.5 to 1.5
- norm_shifts: bfloat16 [4, 1024], P(None, 'dp'), may hold values from -2 to 2
Outputs:
- layer_out: bfloat16 [16384, 1024], P(('dp', 'seq'))
- tokens_grad: bfloat16 [16384, 1024], P(('dp', 'seq'))
- qkv_weight_grad: float32 [1024, 3072], P('dp')
- qv_bias_grad: float32 [2, 1024], P(None, 'dp')
- proj_weight_grad: float32 [1024, 1024], P('dp')
- fc1_weight_grad: float32 [1024, 4096], P('dp')
- fc1_bias_grad: float32 [4096], P('dp')
- fc2_weight_grad: float32 [4096, 1024], P('dp')
- out_bias_grad: float32 [2, 1024], P(None, 'dp')
- norm_gains_grad: float32 [4, 1024], P(None, 'dp')
- norm_shifts_grad: float32 [4, 1024], P(None, 'dp')
All inputs are finite; a program needn't handle non-finite values.
Results may differ from a plain program's by a relative error of at most 0.015.
The roundings to bfloat16 on the way count: a program that leaves them out, or rounds other values in their place, can miss the bound.
Values may be sent and summed in bfloat16 or wider, within the bound.
No kernel may reach another device: no remote copies, remote signals or barrier semaphores. Data moves between devices by JAX's collectives and lax.ppermute only.
A program may use at most 192 MiB of HBM per device.

v0:
```python
from functools import partial
import math
import jax
import jax.numpy as jnp
from jax import lax
from jax.sharding import PartitionSpec as P

HEAD_DIM = 64
RELAX_ALPHA = 32.0
NORM_EPS = 1e-05


def layer_norm(values, gain_vec, shift_vec):
    centred = values - jnp.mean(values, axis=-1, keepdims=True)
    variance = jnp.mean(centred * centred, axis=-1, keepdims=True)
    return centred * lax.rsqrt(variance + NORM_EPS) * gain_vec + shift_vec


def contract_rows(left, right):
    return lax.dot_general(
        left, right, (((0,), (0,)), ((), ())), preferred_element_type=jnp.float32
    )


def contract_cols(left, right):
    return lax.dot_general(
        left, right, (((1,), (1,)), ((), ())), preferred_element_type=jnp.float32
    )


def norm_backward(values, gain_vec, shift_vec, upstream):
    unused_out, pullback = jax.vjp(layer_norm, values, gain_vec, shift_vec)
    return pullback(upstream)


def column_sums(values):
    return jnp.sum(values.astype(jnp.float32), axis=0)


def causal_logits(scores, block_start):
    row_index = block_start + lax.iota(jnp.int32, scores.shape[0])
    col_index = lax.iota(jnp.int32, scores.shape[1])
    return jnp.where(row_index[:, None] >= col_index[None, :], RELAX_ALPHA * scores, -1e30)


def block_layout(seq_len):
    block_rows = min(512, seq_len)
    return (block_rows, seq_len // block_rows)


def head_column(array, head_index):
    return lax.dynamic_index_in_dim(array, head_index, axis=1, keepdims=False)


def head_block(array, head_index, block_start, block_rows):
    piece = lax.dynamic_slice(
        array, (block_start, head_index, jnp.int32(0)), (block_rows, 1, array.shape[2])
    )
    return piece.reshape(block_rows, array.shape[2])


def scale_table():
    query_scale = 1.0 / (RELAX_ALPHA * math.sqrt(HEAD_DIM))
    return jnp.array([query_scale, 1.0, 1.0], jnp.float32)[:, None]


def gather_attention(qkv_weight, qv_bias, proj_weight, out_bias, norm_gains, norm_shifts):
    return (
        lax.all_gather(qkv_weight, "dp", axis=0, tiled=True),
        lax.all_gather(qv_bias, "dp", axis=1, tiled=True),
        lax.all_gather(proj_weight, "dp", axis=0, tiled=True),
        lax.all_gather(out_bias, "dp", axis=1, tiled=True),
        lax.all_gather(norm_gains, "dp", axis=1, tiled=True),
        lax.all_gather(norm_shifts, "dp", axis=1, tiled=True),
    )


def gather_mlp(fc1_weight, fc1_bias, fc2_weight):
    return (
        lax.all_gather(fc1_weight, "dp", axis=0, tiled=True),
        lax.all_gather(fc1_bias, "dp", axis=0, tiled=True),
        lax.all_gather(fc2_weight, "dp", axis=0, tiled=True),
    )


def run_forward(tokens, attn_full, mlp_full):
    qkv_w, qv_b, proj_w, out_b, gains_low, shifts_low = attn_full
    fc1_w, fc1_b, fc2_w = mlp_full
    gain_rows = gains_low.astype(jnp.float32)
    shift_rows = shifts_low.astype(jnp.float32)
    model_width = qkv_w.shape[0]
    tok_rows = tokens.shape[0]
    tok_vals = tokens.astype(jnp.float32)
    normed = layer_norm(tok_vals, gain_rows[0], shift_rows[0]).astype(jnp.bfloat16)
    mixed_cols = jnp.dot(normed, qkv_w, preferred_element_type=jnp.float32).reshape(
        tok_rows, 3, model_width
    )
    bias_rows = qv_b.astype(jnp.float32)
    bias_three = jnp.stack((bias_rows[0], jnp.zeros_like(bias_rows[0]), bias_rows[1]))
    stacked = ((mixed_cols + bias_three) * scale_table()).astype(jnp.bfloat16)
    by_heads = lax.all_to_all(stacked, "seq", split_axis=2, concat_axis=0, tiled=True)
    seq_len = by_heads.shape[0]
    local_heads = by_heads.shape[2] // HEAD_DIM
    head_split = by_heads.reshape(seq_len, 3, local_heads, HEAD_DIM)
    queries = head_split[:, 0]
    key_rows = head_split[:, 1]
    values = head_split[:, 2]
    block_rows, blocks = block_layout(seq_len)

    def one_block(step_index):
        head_index = step_index // blocks
        block_start = step_index % blocks * block_rows
        q_block = head_block(queries, head_index, block_start, block_rows)
        k_head = head_column(key_rows, head_index)
        v_head = head_column(values, head_index)
        scores = contract_cols(q_block, k_head)
        logits = causal_logits(scores, block_start)
        row_top = jnp.max(logits, axis=-1, keepdims=True)
        powers = jnp.exp(logits - row_top)
        row_total = jnp.sum(powers, axis=-1, keepdims=True)
        probs_low = (powers / row_total).astype(jnp.bfloat16)
        out_block = jnp.dot(probs_low, v_head, preferred_element_type=jnp.float32)
        return (out_block.astype(jnp.bfloat16), (row_top + jnp.log(row_total))[:, 0])

    out_blocks, lse_blocks = lax.map(one_block, lax.iota(jnp.int32, local_heads * blocks))
    attended_heads = (
        out_blocks.reshape(local_heads, seq_len, HEAD_DIM)
        .transpose(1, 0, 2)
        .reshape(seq_len, local_heads * HEAD_DIM)
    )
    attended = lax.all_to_all(attended_heads, "seq", split_axis=0, concat_axis=1, tiled=True)
    branch = jnp.dot(attended, proj_w, preferred_element_type=jnp.float32) + out_b[0].astype(
        jnp.float32
    )
    residual = tok_vals + layer_norm(branch, gain_rows[1], shift_rows[1])
    normed_two = layer_norm(residual, gain_rows[2], shift_rows[2]).astype(jnp.bfloat16)
    hidden = jnp.dot(normed_two, fc1_w, preferred_element_type=jnp.float32) + fc1_b.astype(
        jnp.float32
    )
    active = jax.nn.gelu(hidden, approximate=True).astype(jnp.bfloat16)
    second = jnp.dot(active, fc2_w, preferred_element_type=jnp.float32) + out_b[1].astype(
        jnp.float32
    )
    layer_out = residual + layer_norm(second, gain_rows[3], shift_rows[3])
    kept_state = (
        tok_vals,
        normed,
        queries,
        key_rows,
        values,
        lse_blocks,
        attended,
        branch,
        residual,
        normed_two,
        hidden,
        active,
        second,
    )
    return (layer_out, kept_state)


def per_device(
    tokens,
    out_grad,
    qkv_weight,
    qv_bias,
    proj_weight,
    fc1_weight,
    fc1_bias,
    fc2_weight,
    out_bias,
    norm_gains,
    norm_shifts,
):
    attn_full = gather_attention(
        qkv_weight, qv_bias, proj_weight, out_bias, norm_gains, norm_shifts
    )
    mlp_full = gather_mlp(fc1_weight, fc1_bias, fc2_weight)
    layer_out, kept_state = run_forward(tokens, attn_full, mlp_full)
    attn_full = gather_attention(
        qkv_weight, qv_bias, proj_weight, out_bias, norm_gains, norm_shifts
    )
    mlp_full = gather_mlp(fc1_weight, fc1_bias, fc2_weight)
    repeat_out, kept_state = run_forward(tokens, attn_full, mlp_full)
    qkv_w, qv_b, proj_w, out_b, gains_low, shifts_low = attn_full
    fc1_w, fc1_b, fc2_w = mlp_full
    gain_rows = gains_low.astype(jnp.float32)
    shift_rows = shifts_low.astype(jnp.float32)
    (
        tok_vals,
        normed,
        queries,
        key_rows,
        values,
        lse_blocks,
        attended,
        branch,
        residual,
        normed_two,
        hidden,
        active,
        second,
    ) = kept_state
    tok_rows = tok_vals.shape[0]
    model_width = qkv_w.shape[0]
    upstream = out_grad.astype(jnp.float32)
    d_second, grad_gain_three, grad_shift_three = norm_backward(
        second, gain_rows[3], shift_rows[3], upstream
    )
    d_second = d_second.astype(jnp.bfloat16)
    grad_fc2 = contract_rows(active, d_second)
    grad_bias_two = column_sums(d_second)
    d_active = contract_cols(d_second, fc2_w)
    unused_gelu, gelu_back = jax.vjp(partial(jax.nn.gelu, approximate=True), hidden)
    d_hidden = gelu_back(d_active)[0].astype(jnp.bfloat16)
    grad_fc1 = contract_rows(normed_two, d_hidden)
    grad_fc1_bias = column_sums(d_hidden)
    d_normed_two = contract_cols(d_hidden, fc1_w)
    d_resid_part, grad_gain_two, grad_shift_two = norm_backward(
        residual, gain_rows[2], shift_rows[2], d_normed_two
    )
    d_residual = upstream + d_resid_part
    d_branch, grad_gain_one, grad_shift_one = norm_backward(
        branch, gain_rows[1], shift_rows[1], d_residual
    )
    d_branch = d_branch.astype(jnp.bfloat16)
    grad_proj = contract_rows(attended, d_branch)
    grad_bias_one = column_sums(d_branch)
    d_attended = contract_cols(d_branch, proj_w).astype(jnp.bfloat16)
    seq_len = queries.shape[0]
    local_heads = queries.shape[1]
    block_rows, blocks = block_layout(seq_len)
    d_heads = lax.all_to_all(d_attended, "seq", split_axis=1, concat_axis=0, tiled=True).reshape(
        seq_len, local_heads, HEAD_DIM
    )
    zero_grad = jnp.zeros(queries.shape, jnp.float32)

    def back_step(grad_pair, step_index):
        key_grad, value_grad = grad_pair
        head_index = step_index // blocks
        block_start = step_index % blocks * block_rows
        q_block = head_block(queries, head_index, block_start, block_rows)
        d_block = head_block(d_heads, head_index, block_start, block_rows)
        k_head = head_column(key_rows, head_index)
        v_head = head_column(values, head_index)
        scores = contract_cols(q_block, k_head)
        probs = jnp.exp(causal_logits(scores, block_start) - lse_blocks[step_index][:, None])
        d_probs = contract_cols(d_block, v_head)
        row_delta = jnp.sum(probs * d_probs, axis=-1, keepdims=True)
        d_scores = (RELAX_ALPHA * probs * (d_probs - row_delta)).astype(jnp.bfloat16)
        query_grad = jnp.dot(d_scores, k_head, preferred_element_type=jnp.float32)
        key_add = contract_rows(d_scores, q_block)
        value_add = contract_rows(probs.astype(jnp.bfloat16), d_block)
        key_grad = lax.dynamic_update_index_in_dim(
            key_grad, head_column(key_grad, head_index) + key_add, head_index, 1
        )
        value_grad = lax.dynamic_update_index_in_dim(
            value_grad, head_column(value_grad, head_index) + value_add, head_index, 1
        )
        return ((key_grad, value_grad), query_grad.astype(jnp.bfloat16))

    (key_grad, value_grad), query_blocks = lax.scan(
        back_step, (zero_grad, zero_grad), lax.iota(jnp.int32, local_heads * blocks)
    )
    query_grad = query_blocks.reshape(local_heads, seq_len, HEAD_DIM).transpose(1, 0, 2)
    back_stack = jnp.stack(
        (query_grad, key_grad.astype(jnp.bfloat16), value_grad.astype(jnp.bfloat16)), axis=1
    ).reshape(seq_len, 3, local_heads * HEAD_DIM)
    back_tokens = lax.all_to_all(back_stack, "seq", split_axis=0, concat_axis=2, tiled=True)
    d_mixed = (
        (back_tokens.astype(jnp.float32) * scale_table())
        .astype(jnp.bfloat16)
        .reshape(tok_rows, 3 * model_width)
    )
    grad_qkv = contract_rows(normed, d_mixed)
    mixed_sums = column_sums(d_mixed).reshape(3, model_width)
    grad_qv_bias = jnp.stack((mixed_sums[0], mixed_sums[2]))
    d_normed = contract_cols(d_mixed, qkv_w)
    d_tok_part, grad_gain_zero, grad_shift_zero = norm_backward(
        tok_vals, gain_rows[0], shift_rows[0], d_normed
    )
    tokens_grad = (d_residual + d_tok_part).astype(jnp.bfloat16)
    grad_out_bias = jnp.stack((grad_bias_one, grad_bias_two))
    grad_gains = jnp.stack((grad_gain_zero, grad_gain_one, grad_gain_two, grad_gain_three))
    grad_shifts = jnp.stack((grad_shift_zero, grad_shift_one, grad_shift_two, grad_shift_three))
    owned = (
        lax.psum_scatter(grad_qkv, "dp", scatter_dimension=0, tiled=True),
        lax.psum_scatter(grad_qv_bias, "dp", scatter_dimension=1, tiled=True),
        lax.psum_scatter(grad_proj, "dp", scatter_dimension=0, tiled=True),
        lax.psum_scatter(grad_fc1, "dp", scatter_dimension=0, tiled=True),
        lax.psum_scatter(grad_fc1_bias, "dp", scatter_dimension=0, tiled=True),
        lax.psum_scatter(grad_fc2, "dp", scatter_dimension=0, tiled=True),
        lax.psum_scatter(grad_out_bias, "dp", scatter_dimension=1, tiled=True),
        lax.psum_scatter(grad_gains, "dp", scatter_dimension=1, tiled=True),
        lax.psum_scatter(grad_shifts, "dp", scatter_dimension=1, tiled=True),
    )
    totals = (
        lax.psum(owned[0].astype(jnp.bfloat16), "seq").astype(jnp.float32),
        lax.psum(owned[1].astype(jnp.bfloat16), "seq").astype(jnp.float32),
        lax.psum(owned[2].astype(jnp.bfloat16), "seq").astype(jnp.float32),
        lax.psum(owned[3].astype(jnp.bfloat16), "seq").astype(jnp.float32),
        lax.psum(owned[4].astype(jnp.bfloat16), "seq").astype(jnp.float32),
        lax.psum(owned[5].astype(jnp.bfloat16), "seq").astype(jnp.float32),
        lax.psum(owned[6].astype(jnp.bfloat16), "seq").astype(jnp.float32),
        lax.psum(owned[7].astype(jnp.bfloat16), "seq").astype(jnp.float32),
        lax.psum(owned[8].astype(jnp.bfloat16), "seq").astype(jnp.float32),
    )
    return (
        layer_out.astype(jnp.bfloat16),
        tokens_grad,
        totals[0],
        totals[1],
        totals[2],
        totals[3],
        totals[4],
        totals[5],
        totals[6],
        totals[7],
        totals[8],
    )


def solution(mesh):
    placed = (
        P(("dp", "seq"), None),
        P(("dp", "seq"), None),
        P("dp", None),
        P(None, "dp"),
        P("dp", None),
        P("dp", None),
        P("dp"),
        P("dp", None),
        P(None, "dp"),
        P(None, "dp"),
        P(None, "dp"),
    )
    return jax.shard_map(
        per_device,
        mesh=mesh,
        in_specs=placed,
        out_specs=(
            P(("dp", "seq"), None),
            P(("dp", "seq"), None),
            P("dp", None),
            P(None, "dp"),
            P("dp", None),
            P("dp", None),
            P("dp"),
            P("dp", None),
            P(None, "dp"),
            P(None, "dp"),
            P(None, "dp"),
        ),
        check_vma=False,
    )
```

profile of v0, /device:TPU:0, one launch (start us, length us, event | category | flops | bytes accessed | tf_op | source)
XLA Modules:
  0.0 2192.8 jit_solution(13262523268789830104)
XLA Ops:
  9.5 22.3 %all_gather.39 = bf16[2,1024]{1,0:T(2,128)(2,1)S(1)} all-gather(bf16[2,128]{1,0:T(2,128)(2,1)S(1)} %copy-done.48), channel_id=1, replica_groups=mesh['dp'=8,'seq'=4] {'dp'}, dimensions={1}, use_global_device_ids=true | all-gather | bytes 4608 | tf_op jit(solution)/shard_map/all_gather | solution.py:70
  31.8 16.7 all_gather.36
  48.5 18.3 all_gather.37
  69.3 42.9 %all-gather.6.cloned.1.call-done = bf16[1024,3072]{1,0:T(8,128)(2,1)} async-done(((bf16[128,3072]{1,0:T(8,128)(2,1)}), bf16[1024,3072]{1,0:T(8,128)(2,1)}) %all-gather.6.cloned.1.call-update) | async-done | bytes 6291472 | tf_op jit(solution)/shard_map/all_gather | solution.py:69
  112.2 5.9 fusion.95
  118.9 4.7 copy.51
  123.5 4.9 all-to-all-start
  129.0 47.6 %all-to-all-done = bf16[512,3,1024]{0,1,2:T(4,128)(2,1)} async-done(((bf16[512,3,1024]{0,1,2:T(4,128)(2,1)}), bf16[512,3,1024]{0,1,2:T(4,128)(2,1)}, u32[]{:S(2)}, u32[]{:S(2)}) %all-to-all-start) | async-done | bytes 3145760 | tf_op jit(solution)/shard_map/all_to_all | solution.py:101
  179.6 4.1 copy.53
  183.7 6.1 reshape.336
  194.1 119.5 %while.42 = (s32[]{:T(128)}, bf16[16,512,64]{1,2,0:T(8,128)(2,1)}, s32[16]{0:T(128)S(1)}, bf16[2048,4,64]{0,2,1:T(8,128)(2,1)}, bf16[2048,4,64]{0,2,1:T(8,128)(2...) while((s32[]{:T(128)}, bf16[16,512,64]{1,2,0:T(8,128)(2,1)}, ...), condition=%wide.region_5.6_spmd, body=%wide.region_2.5_spmd.sunk | while | flops 277904928 | bytes 13255076 | solution.py:125
  326.7 4.4 all-to-all-start.1
  332.3 174.0 %while.43 = (s32[]{:T(128)}, bf16[16,512,64]{1,2,0:T(8,128)(2,1)}, f32[16,512]{1,0:T(8,128)S(1)}, s32[16]{0:T(128)S(1)}, bf16[2048,4,64]{0,2,1:T(8,128)(2,1)}, /...) while((s32[]{:T(128)}, bf16[16,512,64]{1,2,0:T(8,128)(2,1)}, ...), condition=%wide.region_15.16_spmd, body=%wide.region_12.15_spmd.sunk | while | flops 277905440 | bytes 30042572 | solution.py:125
  339.3 4.4 fusion.172
  519.7 26.0 %all-gather = bf16[8,1,512]{2,1,0:T(2,128)(2,1)S(1)} all-gather(bf16[1,1,512]{2,1,0:T(2,128)(2,1)S(1)} %reshape.355), channel_id=1, replica_groups=mesh['dp'=8,'seq'=4] {'dp'}, dimensions={0}, use_global_device_ids=true | all-gather | bytes 9216 | tf_op jit(solution)/shard_map/all_gather | solution.py:81
  545.7 16.2 all_gather.41
  561.9 4.5 fusion.114
  567.4 4.1 add_reduce_fusion.1
  576.5 11.9 fusion.99
  588.5 12.5 add_reduce_fusion
  601.0 18.2 multiply_reduce_fusion.5
  619.3 4.1 fusion.84
  627.8 16.6 convert_reduce_fusion
  644.4 7.0 multiply_reduce_fusion.1
  666.3 10.5 all-to-all-done.3
  682.2 300.8 %while.44 = (s32[]{:T(128)}, f32[2048,4,64]{0,2,1:T(8,128)S(1)}, f32[2048,4,64]{0,2,1:T(8,128)}, bf16[16,512,64]{1,2,0:T(8,128)(2,1)}, s32[16]{0:T(128)S(1)}, /*...) while((s32[]{:T(128)}, f32[2048,4,64]{0,2,1:T(8,128)S(1)}, ...), condition=%wide.region_30.31_spmd, body=%wide.region_28.30_spmd.sunk | while | flops 682917888 | bytes 53564424 | solution.py:263
  690.4 4.1 multiply_reduce_fusion.12
  709.2 4.0 multiply_reduce_fusion.12
  747.0 4.0 multiply_reduce_fusion.12
  765.8 4.0 multiply_reduce_fusion.12
  990.2 4.8 copy.64
  995.0 5.0 all-to-all-start.4
  1000.2 48.1 %all-to-all-done.4 = bf16[2048,3,256]{2,1,0:T(4,128)(2,1)} async-done(((bf16[2048,3,256]{2,1,0:T(4,128)(2,1)}), bf16[2048,3,256]{2,1,0:T(4,128)(2,1)}, u32[]{:S(2)}, u32[]{:S(2)}) %all-to-all-start.4) | async-done | bytes 3145760 | tf_op jit(solution)/shard_map/all_to_all | solution.py:270
  1054.2 6.6 copy.66
  1066.1 6.9 fusion.93
  1074.6 10.4 fusion.98
  1086.3 15.5 fusion.100
  1103.6 6.9 fusion.102
  1120.6 157.7 %reduce-scatter.17.cloned.1.call-done = f32[128,3072]{1,0:T(8,128)} async-done(((f32[1024,3072]{1,0:T(8,128)}), f32[128,3072]{1,0:T(8,128)}) %reduce-scatter.17.cloned.1.call-update) | async-done | bytes 1572880 | tf_op jit(solution)/shard_map/reduce_scatter | solution.py:288
  1280.7 283.0 %reduce-scatter.21.cloned.1.call-done = f32[128,4096]{1,0:T(8,128)} async-done(((f32[1024,4096]{1,0:T(8,128)}), f32[128,4096]{1,0:T(8,128)}) %reduce-scatter.21.cloned.1.call-update) | async-done | bytes 2097168 | tf_op jit(solution)/shard_map/reduce_scatter | solution.py:291
  1566.4 282.8 %reduce-scatter.23.cloned.1.call-done = f32[512,1024]{1,0:T(8,128)} async-done(((f32[4096,1024]{1,0:T(8,128)}), f32[512,1024]{1,0:T(8,128)}) %reduce-scatter.23.cloned.1.call-update) | async-done | bytes 2097168 | tf_op jit(solution)/shard_map/reduce_scatter | solution.py:293
  1853.8 35.3 %all-reduce = bf16[4096]{0:T(1024)(128)(2,1)S(1)} all-reduce(f32[4096]{0:T(1024)S(1)} %get-tuple-element.399), channel_id=6, replica_groups=mesh['dp'=8,'seq'=4] {'dp'}, use_global_device_ids=true, to_apply=%region_43.44.clone | all-reduce | flops 4096 | bytes 24576
  1889.2 25.3 %reduce-scatter.27.cloned.1.call-done = f32[128,2]{1,0:T(8,128)} async-done(((f32[1024,2]{1,0:T(8,128)}), f32[128,2]{1,0:T(8,128)}) %reduce-scatter.27.cloned.1.call-update) | async-done | bytes 1040
  1918.7 60.5 %reduce-scatter.25.cloned.1.call-done = f32[128,2]{1,0:T(8,128)} async-done(((f32[1024,2]{1,0:T(8,128)}), f32[128,2]{1,0:T(8,128)}) %reduce-scatter.25.cloned.1.call-update) | async-done | bytes 1040
  1980.1 63.8 %reduce-scatter.31.cloned.1.call-done = f32[128,4]{1,0:T(8,128)} async-done(((f32[1024,4]{1,0:T(8,128)}), f32[128,4]{1,0:T(8,128)}) %reduce-scatter.31.cloned.1.call-update) | async-done | bytes 2064
  2044.8 63.3 %reduce-scatter.29.cloned.1.call-done = f32[128,4]{1,0:T(8,128)} async-done(((f32[1024,4]{1,0:T(8,128)}), f32[128,4]{1,0:T(8,128)}) %reduce-scatter.29.cloned.1.call-update) | async-done | bytes 2064
  2109.0 5.7 all-reduce.1
  2117.5 62.0 %all-reduce.5.cloned.1.call-done = (bf16[128,3072]{1,0:T(8,128)(2,1)}, bf16[128,1024]{1,0:T(8,128)(2,1)}, bf16[128,4096]{1,0:T(8,128)(2,1)}, bf16[512,1024]{1,0:T(8,128)(2,1)}) async-done(((bf16[128,3072]{1,0:T(8,128)(2,1)}, bf16[128,1024]{1,0:T(8,128)(2,1)}, bf16[128,4096]{1,0:T(8,128)(2,1)}, bf16[512,1024]{1,0:T(8,128)(2,1)}), (bf16[128,3072]{1,0:T(8,128)(2,1)}, bf16[128,1024]{1,0:T(8,128)(2,1)}, ...) | async-done | bytes 3145744 | tf_op jit(solution)/shard_map/psum | solution.py:299
  (660 shorter events, 555.3 us)
Async XLA Ops:
  7.2 24.6 %copy-start.45 = (bf16[4,128]{1,0:T(4,128)(2,1)S(1)}, bf16[4,128]{1,0:T(4,128)(2,1)}, u32[]{:S(2)}) copy-start(bf16[4,128]{1,0:T(4,128)(2,1)} %param.29) | copy-start | bytes 3076
  7.2 41.3 %copy-start.46 = (bf16[4,128]{1,0:T(4,128)(2,1)S(1)}, bf16[4,128]{1,0:T(4,128)(2,1)}, u32[]{:S(2)}) copy-start(bf16[4,128]{1,0:T(4,128)(2,1)} %param.30) | copy-start | bytes 3076
  7.2 59.6 %copy-start.2 = (bf16[512,1024]{1,0:T(8,128)(2,1)S(1)}, bf16[512,1024]{1,0:T(8,128)(2,1)}, u32[]{:S(2)}) copy-start(bf16[512,1024]{1,0:T(8,128)(2,1)} %param.20) | copy-start | bytes 3145732
  7.2 104.9 %all-gather.6.cloned.1.call-start = ((), (), s32[]{:S(2)}) async-start(), calls=%async_computation.13 | async-start | bytes 7077888 | tf_op jit(solution)/shard_map/all_gather | solution.py:69
  8.0 554.0 %all-gather.8.cloned.1.call-start = ((), (), s32[]{:S(2)}) async-start(), calls=%async_computation.14 | async-start | bytes 2359296 | tf_op jit(solution)/shard_map/all_gather | solution.py:71
  8.7 567.8 %all-gather.10.cloned.1.call-start = ((), (), s32[]{:S(2)}) async-start(), calls=%async_computation.15 | async-start | bytes 9437184 | tf_op jit(solution)/shard_map/all_gather | solution.py:80
  67.0 51.1 %copy-start.31 = (f32[512]{0:T(512)}, f32[512]{0:T(512)S(1)}, u32[]{:S(2)}) copy-start(f32[512]{0:T(512)S(1)} %broadcast_multiply_fusion.6) | copy-start | bytes 6148
  67.5 50.7 %copy-start.33 = (f32[512]{0:T(512)}, f32[512]{0:T(512)S(1)}, u32[]{:S(2)}) copy-start(f32[512]{0:T(512)S(1)} %fusion.89) | copy-start | bytes 6148
  68.7 49.4 %copy-start.29 = (f32[1,1024]{1,0:T(1,128)}, f32[1,1024]{1,0:T(1,128)S(1)}, u32[]{:S(2)}) copy-start(f32[1,1024]{1,0:T(1,128)S(1)} %get-tuple-element.431) | copy-start | bytes 12292
  69.3 48.8 %copy-start.43 = (f32[1,1024]{1,0:T(1,128)}, f32[1,1024]{1,0:T(1,128)S(1)}, u32[]{:S(2)}) copy-start(f32[1,1024]{1,0:T(1,128)S(1)} %get-tuple-element.435) | copy-start | bytes 12292
  112.2 6.0 copy-start.41
  123.5 53.1 %all-to-all-start = ((bf16[512,3,1024]{0,1,2:T(4,128)(2,1)}), bf16[512,3,1024]{0,1,2:T(4,128)(2,1)}, u32[]{:S(2)}, u32[]{:S(2)}) async-start(bf16[512,3,1024]{0,1,2:T(4,128)(2,1)} %copy.51), calls=%async_computation | async-start | bytes 8388608 | tf_op jit(solution)/shard_map/all_to_all | solution.py:101
  128.4 460.1 %all-gather.12.cloned.1.call-start = ((), (), s32[]{:S(2)}) async-start(), calls=%async_computation.16 | async-start | bytes 9437184 | tf_op jit(solution)/shard_map/all_gather | solution.py:82
  326.7 189.4 %all-to-all-start.1 = ((bf16[4,512,256]{1,2,0:T(8,128)(2,1)}), bf16[4,512,256]{1,2,0:T(8,128)(2,1)}, u32[]{:S(2)}, u32[]{:S(2)}) async-start(bf16[4,512,256]{1,2,0:T(8,128)(2,1)} %copy.56), calls=%async_computation.1 | async-start | bytes 2097152 | tf_op jit(solution)/shard_map/all_to_all | solution.py:131
  506.3 6.1 copy-start.13
  506.3 6.1 copy-start.18
  515.0 4.7 copy-start.47
  515.0 30.8 %copy-start.49 = (bf16[2,128]{1,0:T(2,128)(2,1)S(1)}, bf16[2,128]{1,0:T(2,128)(2,1)}, u32[]{:S(2)}) copy-start(bf16[2,128]{1,0:T(2,128)(2,1)} %param.28) | copy-start | bytes 1540
  516.2 50.3 %all-to-all-start.2 = ((bf16[4,512,256]{1,2,0:T(8,128)(2,1)}), bf16[4,512,256]{1,2,0:T(8,128)(2,1)S(1)}, u32[]{:S(2)}, u32[]{:S(2)}) async-start(bf16[4,512,256]{1,2,0:T(8,128)(2,1)} %copy.59), calls=%async_computation.2 | async-start | bytes 2097152 | tf_op jit(solution)/shard_map/all_to_all | solution.py:131
  601.0 18.2 copy-start.15
  601.0 18.2 copy-start.28
  619.2 4.2 copy-start.12
  626.9 17.4 slice-start
  627.8 16.6 copy-start.22
  627.8 16.6 copy-start.8
  627.8 16.6 slice-start.1
  657.5 5.4 copy-start.25
  658.9 18.0 all-to-all-start.3
  662.4 456.4 %reduce-scatter.19.cloned.1.call-start = ((), (), s32[]{:S(2)}) async-start(), calls=%async_computation.18 | async-start | bytes 4718592 | tf_op jit(solution)/shard_map/reduce_scatter | solution.py:290
  995.0 5.1 copy-start.42
  995.0 53.2 %all-to-all-start.4 = ((bf16[2048,3,256]{2,1,0:T(4,128)(2,1)}), bf16[2048,3,256]{2,1,0:T(4,128)(2,1)}, u32[]{:S(2)}, u32[]{:S(2)}) async-start(bf16[2048,3,256]{2,1,0:T(4,128)(2,1)} %copy.64), calls=%async_computation.4 | async-start | bytes 8388608 | tf_op jit(solution)/shard_map/all_to_all | solution.py:270
  1000.0 278.3 %reduce-scatter.17.cloned.1.call-start = ((), (), s32[]{:S(2)}) async-start(), calls=%async_computation.17 | async-start | bytes 14155776 | tf_op jit(solution)/shard_map/reduce_scatter | solution.py:288
  1060.8 5.3 copy-start.3
  1060.8 5.3 copy-start.30
  1060.8 5.3 copy-start.32
  1060.8 5.3 copy-start.34
  1060.8 5.3 copy-start.44
  1073.0 490.7 %reduce-scatter.21.cloned.1.call-start = ((), (), s32[]{:S(2)}) async-start(), calls=%async_computation.19 | async-start | bytes 18874368 | tf_op jit(solution)/shard_map/reduce_scatter | solution.py:291
  1085.1 764.1 %reduce-scatter.23.cloned.1.call-start = ((), (), s32[]{:S(2)}) async-start(), calls=%async_computation.20 | async-start | bytes 18874368 | tf_op jit(solution)/shard_map/reduce_scatter | solution.py:293
  1101.8 812.7 %reduce-scatter.27.cloned.1.call-start = ((), (), s32[]{:S(2)}) async-start(), calls=%async_computation.22 | async-start | bytes 589824
  1103.5 7.0 copy-start.36
  1103.5 875.7 %reduce-scatter.25.cloned.1.call-start = ((), (), s32[]{:S(2)}) async-start(), calls=%async_computation.21 | async-start | bytes 589824
  1110.5 6.1 copy-start.16
  1110.6 4.9 copy-start.40
  1115.4 928.5 %reduce-scatter.31.cloned.1.call-start = ((), (), s32[]{:S(2)}) async-start(), calls=%async_computation.24 | async-start | bytes 589824
  1116.6 991.5 %reduce-scatter.29.cloned.1.call-start = ((), (), s32[]{:S(2)}) async-start(), calls=%async_computation.23 | async-start | bytes 589824
  1118.7 1060.8 %all-reduce.5.cloned.1.call-start = ((), (), s32[]{:S(2)}) async-start(), calls=%async_computation.25 | async-start | bytes 6291456 | tf_op jit(solution)/shard_map/psum | solution.py:299
  1851.9 63.5 %copy-start.6 = (f32[512,1024]{1,0:T(8,128)S(1)}, f32[512,1024]{1,0:T(8,128)}, u32[]{:S(2)}) copy-start(f32[512,1024]{1,0:T(8,128)} %copy-done.5) | copy-start | bytes 6291460
  (53 other events, 136.8 us)
Sparse Core Ops, SparseCore 0:
  10.2 101.8 all-gather.5
  114.3 47.4 all-gather.7
  163.9 123.3 all-gather.9
  289.3 123.6 all-gather.11
  666.6 87.0 reduce-scatter.18
  1073.2 205.0 reduce-scatter.16
  1282.5 281.1 reduce-scatter.20
  1567.5 281.6 reduce-scatter.22
  1853.5 61.0 reduce-scatter.26
  1918.3 60.9 reduce-scatter.24
  1983.0 60.9 reduce-scatter.30
  2047.1 60.9 reduce-scatter.28
  2111.4 68.0 all-reduce.4
where the time goes:
time: 2210 us; the launch traced here: 2190 us
  waiting for transfers between devices  1150 us (52%)
  matrix products  473 us (21%)
  local copies, waits for them, and re-layouts  160 us (7%)
  loops' own time  148 us (7%)
  blocking collectives  140 us (6%)
  other arithmetic  82.9 us (4%)
  starting transfers between devices  22.7 us (1%)
    reduce_scatter x1, waiting for transfers between devices, per_device(): lax.psum_scatter(grad_fc1, 'dp', scatter_dimension=0, tiled=True)  283 us
    reduce_scatter x1, waiting for transfers between devices, per_device(): lax.psum_scatter(grad_fc2, 'dp', scatter_dimension=0, tiled=True)  283 us
    unnamed x17, waiting for transfers between devices  215 us
    dot_general x68, matrix products, contract_cols(): lax.dot_general(left, right, (((1,), (1,)), ((), ())), preferred_element_...  214 us
    reduce_scatter x1, waiting for transfers between devices, per_device(): lax.psum_scatter(grad_qkv, 'dp', scatter_dimension=0, tiled=True)  158 us
    dot_general x36, matrix products, contract_rows(): lax.dot_general(left, right, (((0,), (0,)), ((), ())), preferred_element_...  92.6 us
    dot_general x32, matrix products, one_block(): out_block = jnp.dot(probs_low, v_head, preferred_element_type=jnp.float32)  87.1 us
    another operation x2, loops' own time, run_forward(): lax.map(one_block, lax.iota(jnp.int32, local_heads * blocks))  84.9 us
  transfers between devices with their start and end apart: 18, of which 12 were waited for; matrix products, arithmetic and copies ran while one was open for 28% of the time, Pallas kernels for 0%

commit v1 on v0

--- a/solution.py
+++ b/solution.py
@@ -267,7 +267,10 @@
     back_stack = jnp.stack(
         (query_grad, key_grad.astype(jnp.bfloat16), value_grad.astype(jnp.bfloat16)), axis=1
     ).reshape(seq_len, 3, local_heads * HEAD_DIM)
-    back_tokens = lax.all_to_all(back_stack, "seq", split_axis=0, concat_axis=2, tiled=True)
+    back_tokens = jnp.concatenate(
+        lax.all_to_all(jnp.stack(jnp.split(back_stack, lax.axis_size("seq"), axis=0)), "seq", 0, 0),
+        axis=2,
+    )
     d_mixed = (
         (back_tokens.astype(jnp.float32) * scale_table())
         .astype(jnp.bfloat16)

time: 2210 us -> 2610 us (1.18)
  local copies, waits for them, and re-layouts: 160 us -> 538 us
  matrix products: 473 us -> 504 us
    dynamic_update_slice x0 -> x64, local copies, waits for them, and re-layouts: none -> 348 us  [the longest x32 174 us: back_step(): lax.dynamic_update_index_in_dim(value_grad, head_column(value_grad, head_...]
    dynamic_slice x16, local copies, waits for them, and re-layouts: 18 us -> 53.6 us  [head_column(): return lax.dynamic_index_in_dim(array, head_index, axis=1, keepdims=False)]
  transfers between devices with their start and end apart: 18 -> 18, of which waited for: 12 -> 12; matrix products, arithmetic and copies ran while one was open for 28% -> 38% of each run, Pallas kernels for 0% -> 0%
where the time goes in v1:
time: 2610 us; the launch traced here: 2590 us
  waiting for transfers between devices  1140 us (44%)
  local copies, waits for them, and re-layouts  538 us (21%)
  matrix products  504 us (19%)
  loops' own time  149 us (6%)
  blocking collectives  141 us (5%)
  other arithmetic  81.9 us (3%)
    reduce_scatter x1, waiting for transfers between devices, per_device(): lax.psum_scatter(grad_fc1, 'dp', scatter_dimension=0, tiled=True)  283 us
    reduce_scatter x1, waiting for transfers between devices, per_device(): lax.psum_scatter(grad_fc2, 'dp', scatter_dimension=0, tiled=True)  283 us
    dot_general x68, matrix products, contract_cols(): lax.dot_general(left, right, (((1,), (1,)), ((), ())), preferred_element_...  223 us
    unnamed x17, waiting for transfers between devices  215 us
    dynamic_update_slice x32, local copies, waits for them, and re-layouts, back_step(): lax.dynamic_update_index_in_dim(value_grad, head_column(value_grad, head_...  174 us
    dynamic_update_slice x32, local copies, waits for them, and re-layouts, back_step(): lax.dynamic_update_index_in_dim(key_grad, head_column(key_grad, head_inde...  174 us
    reduce_scatter x1, waiting for transfers between devices, per_device(): lax.psum_scatter(grad_qkv, 'dp', scatter_dimension=0, tiled=True)  156 us
    dot_general x36, matrix products, contract_rows(): lax.dot_general(left, right, (((0,), (0,)), ((), ())), preferred_element_...  106 us
  transfers between devices with their start and end apart: 18, of which 12 were waited for; matrix products, arithmetic and copies ran while one was open for 38% of the time, Pallas kernels for 0%

profile of v1, /device:TPU:0, one launch (start us, length us, event | category | flops | bytes accessed | tf_op | source)
XLA Modules:
  0.0 2588.3 jit_solution(14347033223160631996)
XLA Ops:
  9.5 22.3 all_gather.39
  31.8 16.7 all_gather.36
  48.5 18.3 all_gather.37
  69.3 42.9 %all-gather.6.cloned.1.call-done = bf16[1024,3072]{1,0:T(8,128)(2,1)} async-done(((bf16[128,3072]{1,0:T(8,128)(2,1)}), bf16[1024,3072]{1,0:T(8,128)(2,1)}) %all-gather.6.cloned.1.call-update) | async-done | bytes 6291472 | tf_op jit(solution)/shard_map/all_gather | solution.py:69
  129.0 47.6 %all-to-all-done = bf16[512,3,1024]{0,1,2:T(4,128)(2,1)} async-done(((bf16[512,3,1024]{0,1,2:T(4,128)(2,1)}), bf16[512,3,1024]{0,1,2:T(4,128)(2,1)}, u32[]{:S(2)}, u32[]{:S(2)}) %all-to-all-start) | async-done | bytes 3145760 | tf_op jit(solution)/shard_map/all_to_all | solution.py:101
  193.7 127.3 %while.42 = (s32[]{:T(128)}, bf16[16,512,64]{1,2,0:T(8,128)(2,1)S(1)}, s32[16]{0:T(128)S(1)}, bf16[2048,4,64]{0,2,1:T(8,128)(2,1)}, bf16[2048,4,64]{0,2,1:T(8,12...) while((s32[]{:T(128)}, ...), condition=%wide.region_5.6_spmd, body=%wide.region_2.5_spmd.sunk | while | flops 277904928 | bytes 13255076 | solution.py:125
  329.0 166.2 %while.43 = (s32[]{:T(128)}, bf16[16,512,64]{1,2,0:T(8,128)(2,1)S(1)}, f32[16,512]{1,0:T(8,128)S(1)}, s32[16]{0:T(128)S(1)}, bf16[2048,4,64]{0,2,1:T(8,128)(2,1)...) while((s32[]{:T(128)}, ...), condition=%wide.region_15.16_spmd, body=%wide.region_12.15_spmd.sunk | while | flops 277905440 | bytes 30042572 | solution.py:125
  506.6 26.0 %all-gather = bf16[8,1,512]{2,1,0:T(2,128)(2,1)S(1)} all-gather(bf16[1,1,512]{2,1,0:T(2,128)(2,1)S(1)} %reshape.353), channel_id=1, replica_groups=mesh['dp'=8,'seq'=4] {'dp'}, dimensions={0}, use_global_device_ids=true | all-gather | bytes 9216 | tf_op jit(solution)/shard_map/all_gather | solution.py:81
  532.7 16.5 all_gather.41
  563.3 11.9 fusion.97
  575.2 12.5 add_reduce_fusion
  587.7 18.2 multiply_reduce_fusion.5
  614.6 17.3 convert_reduce_fusion
  653.5 10.8 all-to-all-done.3
  671.6 732.8 %while.44 = (s32[]{:T(128)}, f32[2048,4,64]{0,1,2:T(4,128)}, f32[2048,4,64]{0,1,2:T(4,128)}, bf16[16,512,64]{1,2,0:T(8,128)(2,1)}, s32[16]{0:T(128)S(1)}, /*inde...) while((s32[]{:T(128)}, f32[2048,4,64]{0,1,2:T(4,128)}, ...), condition=%wide.region_30.31_spmd, body=%wide.region_28.30_spmd.sunk | while | flops 682917888 | bytes 74532912 | solution.py:263
  691.2 10.3 dynamic_update_slice.52
  704.9 10.3 dynamic_update_slice.53
  737.2 10.3 dynamic_update_slice.52
  750.8 10.3 dynamic_update_slice.53
  783.0 10.3 dynamic_update_slice.52
  796.6 10.3 dynamic_update_slice.53
  828.8 10.3 dynamic_update_slice.52
  842.4 10.3 dynamic_update_slice.53
  874.5 10.3 dynamic_update_slice.52
  888.2 10.3 dynamic_update_slice.53
  933.9 10.3 dynamic_update_slice.53
  979.7 10.3 dynamic_update_slice.53
  1025.5 10.3 dynamic_update_slice.53
  1071.2 10.3 dynamic_update_slice.53
  1117.0 10.3 dynamic_update_slice.53
  1162.8 10.3 dynamic_update_slice.53
  1208.6 10.3 dynamic_update_slice.53
  1254.3 10.3 dynamic_update_slice.53
  1300.1 10.3 dynamic_update_slice.53
  1345.9 10.3 dynamic_update_slice.53
  1391.7 10.3 dynamic_update_slice.53
  1420.7 36.8 %all-to-all-done.4 = bf16[4,512,3,256]{1,3,2,0:T(8,128)(2,1)S(1)} async-done(((bf16[4,512,3,256]{1,3,2,0:T(8,128)(2,1)}), bf16[4,512,3,256]{1,3,2,0:T(8,128)(2,1)S(1)}, u32[]{:S(2)}, u32[]{:S(2)}) %all-to-all-start.4) | async-done | bytes 3145760 | tf_op jit(solution)/shard_map/all_to_all | solution.py:271
  1469.1 13.3 fusion.96
  1482.9 15.6 fusion.98
  1518.2 155.7 %reduce-scatter.17.cloned.1.call-done = f32[128,3072]{1,0:T(8,128)} async-done(((f32[1024,3072]{1,0:T(8,128)}), f32[128,3072]{1,0:T(8,128)}) %reduce-scatter.17.cloned.1.call-update) | async-done | bytes 1572880 | tf_op jit(solution)/shard_map/reduce_scatter | solution.py:291
  1676.4 282.9 %reduce-scatter.21.cloned.1.call-done = f32[128,4096]{1,0:T(8,128)} async-done(((f32[1024,4096]{1,0:T(8,128)}), f32[128,4096]{1,0:T(8,128)}) %reduce-scatter.21.cloned.1.call-update) | async-done | bytes 2097168 | tf_op jit(solution)/shard_map/reduce_scatter | solution.py:294
  1962.0 282.9 %reduce-scatter.23.cloned.1.call-done = f32[512,1024]{1,0:T(8,128)} async-done(((f32[4096,1024]{1,0:T(8,128)}), f32[512,1024]{1,0:T(8,128)}) %reduce-scatter.23.cloned.1.call-update) | async-done | bytes 2097168 | tf_op jit(solution)/shard_map/reduce_scatter | solution.py:296
  2249.5 35.2 %all-reduce = bf16[4096]{0:T(1024)(128)(2,1)S(1)} all-reduce(f32[4096]{0:T(1024)S(1)} %copy-done.39), channel_id=6, replica_groups=mesh['dp'=8,'seq'=4] {'dp'}, use_global_device_ids=true, to_apply=%region_43.44.clone | all-reduce | flops 4096 | bytes 24576
  2284.8 25.4 reduce-scatter.27.cloned.1.call-done
  2314.4 60.5 %reduce-scatter.25.cloned.1.call-done = f32[128,2]{1,0:T(8,128)} async-done(((f32[1024,2]{1,0:T(8,128)}), f32[128,2]{1,0:T(8,128)}) %reduce-scatter.25.cloned.1.call-update) | async-done | bytes 1040
  2375.7 63.7 %reduce-scatter.31.cloned.1.call-done = f32[128,4]{1,0:T(8,128)} async-done(((f32[1024,4]{1,0:T(8,128)}), f32[128,4]{1,0:T(8,128)}) %reduce-scatter.31.cloned.1.call-update) | async-done | bytes 2064
  2440.4 63.2 %reduce-scatter.29.cloned.1.call-done = f32[128,4]{1,0:T(8,128)} async-done(((f32[1024,4]{1,0:T(8,128)}), f32[128,4]{1,0:T(8,128)}) %reduce-scatter.29.cloned.1.call-update) | async-done | bytes 2064
  2513.1 62.0 %all-reduce.5.cloned.1.call-done = (bf16[128,3072]{1,0:T(8,128)(2,1)}, bf16[128,1024]{1,0:T(8,128)(2,1)}, bf16[128,4096]{1,0:T(8,128)(2,1)}, bf16[512,1024]{1,0:T(8,128)(2,1)}) async-done(((bf16[128,3072]{1,0:T(8,128)(2,1)}, bf16[128,1024]{1,0:T(8,128)(2,1)}, bf16[128,4096]{1,0:T(8,128)(2,1)}, bf16[512,1024]{1,0:T(8,128)(2,1)}), (bf16[128,3072]{1,0:T(8,128)(2,1)}, bf16[128,1024]{1,0:T(8,128)(2,1)}, ...) | async-done | bytes 3145744 | tf_op jit(solution)/shard_map/psum | solution.py:302
  (753 shorter events, 848.2 us)
Async XLA Ops:
  7.2 24.6 copy-start.44
  7.2 41.3 %copy-start.45 = (bf16[4,128]{1,0:T(4,128)(2,1)S(1)}, bf16[4,128]{1,0:T(4,128)(2,1)}, u32[]{:S(2)}) copy-start(bf16[4,128]{1,0:T(4,128)(2,1)} %param.30) | copy-start | bytes 3076
  7.2 59.6 %copy-start.3 = (bf16[512,1024]{1,0:T(8,128)(2,1)S(1)}, bf16[512,1024]{1,0:T(8,128)(2,1)}, u32[]{:S(2)}) copy-start(bf16[512,1024]{1,0:T(8,128)(2,1)} %param.20) | copy-start | bytes 3145732
  7.2 104.9 %all-gather.6.cloned.1.call-start = ((), (), s32[]{:S(2)}) async-start(), calls=%async_computation.13 | async-start | bytes 7077888 | tf_op jit(solution)/shard_map/all_gather | solution.py:69
  8.0 541.2 %all-gather.8.cloned.1.call-start = ((), (), s32[]{:S(2)}) async-start(), calls=%async_computation.14 | async-start | bytes 2359296 | tf_op jit(solution)/shard_map/all_gather | solution.py:71
  8.7 554.6 %all-gather.10.cloned.1.call-start = ((), (), s32[]{:S(2)}) async-start(), calls=%async_computation.15 | async-start | bytes 9437184 | tf_op jit(solution)/shard_map/all_gather | solution.py:80
  67.0 51.1 %copy-start.29 = (f32[512]{0:T(512)}, f32[512]{0:T(512)S(1)}, u32[]{:S(2)}) copy-start(f32[512]{0:T(512)S(1)} %broadcast_multiply_fusion.6) | copy-start | bytes 6148
  67.5 50.7 %copy-start.31 = (f32[512]{0:T(512)}, f32[512]{0:T(512)S(1)}, u32[]{:S(2)}) copy-start(f32[512]{0:T(512)S(1)} %fusion.87) | copy-start | bytes 6148
  68.7 49.4 %copy-start.27 = (f32[1,1024]{1,0:T(1,128)}, f32[1,1024]{1,0:T(1,128)S(1)}, u32[]{:S(2)}) copy-start(f32[1,1024]{1,0:T(1,128)S(1)} %get-tuple-element.435) | copy-start | bytes 12292
  69.3 48.8 %copy-start.42 = (f32[1,1024]{1,0:T(1,128)}, f32[1,1024]{1,0:T(1,128)S(1)}, u32[]{:S(2)}) copy-start(f32[1,1024]{1,0:T(1,128)S(1)} %get-tuple-element.439) | copy-start | bytes 12292
  112.2 6.0 copy-start.40
  123.5 53.1 %all-to-all-start = ((bf16[512,3,1024]{0,1,2:T(4,128)(2,1)}), bf16[512,3,1024]{0,1,2:T(4,128)(2,1)}, u32[]{:S(2)}, u32[]{:S(2)}) async-start(bf16[512,3,1024]{0,1,2:T(4,128)(2,1)} %copy.57), calls=%async_computation | async-start | bytes 8388608 | tf_op jit(solution)/shard_map/all_to_all | solution.py:101
  128.4 446.8 %all-gather.12.cloned.1.call-start = ((), (), s32[]{:S(2)}) async-start(), calls=%async_computation.16 | async-start | bytes 9437184 | tf_op jit(solution)/shard_map/all_gather | solution.py:82
  324.9 178.2 %all-to-all-start.1 = ((bf16[4,512,256]{1,2,0:T(8,128)(2,1)}), bf16[4,512,256]{1,2,0:T(8,128)(2,1)S(1)}, u32[]{:S(2)}, u32[]{:S(2)}) async-start(bf16[4,512,256]{1,2,0:T(8,128)(2,1)} %copy.62), calls=%async_computation.1 | async-start | bytes 2097152 | tf_op jit(solution)/shard_map/all_to_all | solution.py:131
  501.9 4.7 copy-start.46
  501.9 30.8 %copy-start.48 = (bf16[2,128]{1,0:T(2,128)(2,1)S(1)}, bf16[2,128]{1,0:T(2,128)(2,1)}, u32[]{:S(2)}) copy-start(bf16[2,128]{1,0:T(2,128)(2,1)} %param.28) | copy-start | bytes 1540
  503.1 50.3 %all-to-all-start.2 = ((bf16[4,512,256]{1,2,0:T(8,128)(2,1)}), bf16[4,512,256]{1,2,0:T(8,128)(2,1)S(1)}, u32[]{:S(2)}, u32[]{:S(2)}) async-start(bf16[4,512,256]{1,2,0:T(8,128)(2,1)} %copy.65), calls=%async_computation.2 | async-start | bytes 2097152 | tf_op jit(solution)/shard_map/all_to_all | solution.py:131
  554.4 4.1 copy-start.12
  587.7 18.3 copy-start.15
  587.7 18.3 copy-start.26
  606.0 4.2 copy-start.14
  606.0 4.2 copy-start.16
  606.0 4.2 copy-start.38
  613.7 18.1 slice-start
  614.6 17.3 copy-start.21
  614.6 17.3 copy-start.11
  614.6 17.3 slice-start.1
  645.0 5.1 copy-start.23
  646.3 18.0 all-to-all-start.3
  649.9 866.5 %reduce-scatter.19.cloned.1.call-start = ((), (), s32[]{:S(2)}) async-start(), calls=%async_computation.18 | async-start | bytes 4718592 | tf_op jit(solution)/shard_map/reduce_scatter | solution.py:293
  679.8 4.2 copy-start.1
  725.9 4.1 copy-start.1
  771.7 4.1 copy-start.1
  817.5 4.1 copy-start.1
  909.0 4.1 copy-start.1
  1046.3 4.1 copy-start.1
  1229.4 4.1 copy-start.1
  1416.7 40.7 %all-to-all-start.4 = ((bf16[4,512,3,256]{1,3,2,0:T(8,128)(2,1)}), bf16[4,512,3,256]{1,3,2,0:T(8,128)(2,1)S(1)}, u32[]{:S(2)}, u32[]{:S(2)}) async-start(bf16[4,512,3,256]{1,3,2,0:T(8,128)(2,1)} %pad_maximum_fusion.1), calls=%async_computation.4 | async-start | bytes 6291456 | tf_op jit(solution)/shard_map/all_to_all | solution.py:271
  1420.6 253.4 %reduce-scatter.17.cloned.1.call-start = ((), (), s32[]{:S(2)}) async-start(), calls=%async_computation.17 | async-start | bytes 14155776 | tf_op jit(solution)/shard_map/reduce_scatter | solution.py:291
  1469.1 490.2 %reduce-scatter.21.cloned.1.call-start = ((), (), s32[]{:S(2)}) async-start(), calls=%async_computation.19 | async-start | bytes 18874368 | tf_op jit(solution)/shard_map/reduce_scatter | solution.py:294
  1482.4 762.5 %reduce-scatter.23.cloned.1.call-start = ((), (), s32[]{:S(2)}) async-start(), calls=%async_computation.20 | async-start | bytes 18874368 | tf_op jit(solution)/shard_map/reduce_scatter | solution.py:296
  1498.6 811.6 %reduce-scatter.27.cloned.1.call-start = ((), (), s32[]{:S(2)}) async-start(), calls=%async_computation.22 | async-start | bytes 589824
  1500.3 9.1 copy-start.34
  1500.3 874.5 %reduce-scatter.25.cloned.1.call-start = ((), (), s32[]{:S(2)}) async-start(), calls=%async_computation.21 | async-start | bytes 589824
  1511.2 928.2 %reduce-scatter.31.cloned.1.call-start = ((), (), s32[]{:S(2)}) async-start(), calls=%async_computation.24 | async-start | bytes 589824
  1512.4 991.2 %reduce-scatter.29.cloned.1.call-start = ((), (), s32[]{:S(2)}) async-start(), calls=%async_computation.23 | async-start | bytes 589824
  1516.1 1058.9 %all-reduce.5.cloned.1.call-start = ((), (), s32[]{:S(2)}) async-start(), calls=%async_computation.25 | async-start | bytes 6291456 | tf_op jit(solution)/shard_map/psum | solution.py:302
  2247.7 63.4 %copy-start.9 = (f32[512,1024]{1,0:T(8,128)S(1)}, f32[512,1024]{1,0:T(8,128)}, u32[]{:S(2)}) copy-start(f32[512,1024]{1,0:T(8,128)} %copy-done.8) | copy-start | bytes 6291460
  (67 other events, 154.5 us)
Sparse Core Ops, SparseCore 0:
  10.2 101.8 all-gather.5
  114.3 47.4 all-gather.7
  163.9 123.3 all-gather.9
  289.3 123.1 all-gather.11
  654.0 86.9 reduce-scatter.18
  1469.2 204.7 reduce-scatter.16
  1678.2 281.0 reduce-scatter.20
  1963.1 281.7 reduce-scatter.22
  2249.2 60.9 reduce-scatter.26
  2313.9 60.8 reduce-scatter.24
  2378.5 60.8 reduce-scatter.30
  2442.7 60.8 reduce-scatter.28
  2507.0 67.9 all-reduce.4
